TPU v7x, 256 devices: a whole 4x4x8 slice. The times are simulated.
256 devices in a mesh: dom: 32 (over y_lo, z, core), repl: 8 (over y_hi, x).
Axes of the slice: x: 4, y: 4 (y_hi: 2, y_lo: 2; y = y_hi * 2 + y_lo), z: 8, core: 2. Of those that a mesh axis runs over, the one named last changes fastest.
Arguments:
- features: float32 [131072, 256], P(('dom', 'repl')), may hold values from -6 to 6
- weight: bfloat16 [256, 256], replicated, may hold values from -0.375 to 0.375
- bias_vector: float32 [256], replicated, may hold values from -0.5 to 0.5
- cotangent: bfloat16 [131072, 256], P(('dom', 'repl')), may hold values from -6 to 6
- near_tiles: bfloat16 [4096, 128, 128], P(('dom', 'repl')), may hold values from -0.1875 to 0.1875
- near_offsets: int32 [256, 33], P(('dom', 'repl')), may hold values from 0 to 16, as said below
- near_cols: int32 [256, 16], P(('dom', 'repl')), may hold values from 0 to 3, as said below
- far_tiles: bfloat16 [256, 32, 1, 128, 128], P(('dom', 'repl')), may hold values from -0.1875 to 0.1875
- far_rows: int32 [256, 32, 1], P(('dom', 'repl')), may hold values from -1 to 31, as said below
- far_cols: int32 [256, 32, 1], P(('dom', 'repl')), may hold values from 0 to 3
Outputs:
- hidden: bfloat16 [131072, 256], P(('dom', 'repl'))
- grad_features: float32 [131072, 256], P(('dom', 'repl'))
- weight_grad: float32 [256, 256], replicated
Inputs may be any that keep to these rules, and one draw needn't show every extreme that they name: `near_offsets`: each row is non-decreasing, begins with 0 and ends with 16. `near_cols`: within one tile row of one device the near tiles' columns differ and rise. `far_rows`: -1 marks an empty slot. A device's slots for the groups whose index of dom lies at most 2 steps from its own around the cycle are never empty.
All inputs are finite; a program needn't handle non-finite values.
Results may differ from a plain program's by a relative error of at most 0.0075.
Values may be sent and summed in bfloat16 or wider, within the bound.
No kernel may reach another device: no remote copies, remote signals or barrier semaphores. Data moves between devices by JAX's collectives and lax.ppermute only.
A program may use at most 128 MiB of HBM per device.

v0:
```python
import math
import jax
import jax.numpy as jnp
from jax import lax
from jax.sharding import PartitionSpec as P


def membership_flags(index, extent, dtype):
    return (index[..., None] == jnp.arange(extent, dtype=jnp.int32)).astype(dtype)


def slot_rows(offsets, slot_count):
    slots = jnp.arange(slot_count, dtype=jnp.int32)
    return jnp.sum((offsets[1:, None] <= slots[None, :]).astype(jnp.int32), axis=0)


def precise_total_sum(form, hot, values):
    return jnp.einsum(form, hot, values, precision=lax.Precision.HIGHEST)


def select(form, hot, values):
    return jnp.einsum(form, hot, values, preferred_element_type=jnp.float32).astype(jnp.bfloat16)


def tile_product(form, tiles, values):
    return jnp.einsum(form, tiles, values, preferred_element_type=jnp.float32)


def activation_grad(pre_values, upstream):
    sigma = jax.nn.sigmoid(pre_values)
    return (upstream.astype(jnp.float32) * sigma * (1.0 + pre_values * (1.0 - sigma))).astype(
        jnp.bfloat16
    )


def on_device(
    features,
    weight,
    bias_vector,
    cotangent,
    near_tiles,
    near_offsets,
    near_cols,
    far_tiles,
    far_rows,
    far_cols,
):
    rows_dev, feat_width = features.shape
    tile_size = near_tiles.shape[1]
    blocks_per_processor = rows_dev // tile_size
    dom_count = lax.axis_size("dom")
    repl_count = lax.axis_size("repl")
    blocks_dom = blocks_per_processor * repl_count
    near_count = near_tiles.shape[0]
    far_block = far_tiles[0]
    far_row_ids = far_rows[0]
    far_col_ids = far_cols[0]
    near_row_ids = slot_rows(near_offsets[0], near_count)
    nearby_column_index = near_cols[0]
    reduced = features.astype(jnp.bfloat16)
    local_block_list = reduced.reshape(blocks_per_processor, tile_size, feat_width)
    nearby_input_rows = select(
        "el,lxh->exh",
        membership_flags(nearby_column_index, blocks_per_processor, jnp.bfloat16),
        local_block_list,
    )
    near_prod = tile_product("qab,qbf->qaf", near_tiles, nearby_input_rows)
    partial_sum = precise_total_sum(
        "qr,qaf->raf", membership_flags(near_row_ids, blocks_dom, jnp.float32), near_prod
    )
    shard_rows = lax.all_gather(reduced, "dom", axis=0, tiled=True)
    range_count = shard_rows.shape[0] // rows_dev
    tiles = far_block
    row_ids = far_row_ids
    col_ids = far_col_ids
    source = shard_rows.reshape(range_count, blocks_per_processor, tile_size, feat_width)
    inputs = select(
        "kqc,kcbf->kqbf", membership_flags(col_ids, blocks_per_processor, jnp.bfloat16), source
    )
    far_prod = tile_product("kqab,kqbf->kqaf", tiles, inputs)
    partial_sum = partial_sum + precise_total_sum(
        "kqr,kqaf->raf", membership_flags(row_ids, blocks_dom, jnp.float32), far_prod
    )
    group_partial = partial_sum.reshape(blocks_dom * tile_size, feat_width)
    summed = lax.psum_scatter(group_partial, "repl", scatter_dimension=0, tiled=True).astype(
        jnp.bfloat16
    )
    pre_act = jnp.dot(summed, weight, preferred_element_type=jnp.float32) + bias_vector
    hidden = jax.nn.silu(pre_act).astype(jnp.bfloat16)
    grad_pre = activation_grad(pre_act, cotangent)
    weight_term = lax.dot_general(
        summed, grad_pre, (((0,), (0,)), ((), ())), preferred_element_type=jnp.float32
    )
    grad_rows = lax.dot_general(
        grad_pre, weight, (((1,), (1,)), ((), ())), preferred_element_type=jnp.float32
    ).astype(jnp.bfloat16)
    group_grad = lax.all_gather(grad_rows, "repl", axis=0, tiled=True)
    node_total = rows_dev * dom_count * repl_count
    weight_grad = lax.psum(weight_term, ("dom", "repl")) * (1.0 / math.sqrt(node_total))
    cluster_block_list = group_grad.reshape(blocks_dom, tile_size, feat_width)
    near_grads = select(
        "om,mgh->ogh", membership_flags(near_row_ids, blocks_dom, jnp.bfloat16), cluster_block_list
    )
    nearby_backward_pass = tile_product("ltp,ltk->lpk", near_tiles, near_grads)
    local_contribution = precise_total_sum(
        "ml,mrx->lrx",
        membership_flags(nearby_column_index, blocks_per_processor, jnp.float32),
        nearby_backward_pass,
    )
    row_count = rows_dev * lax.axis_size("dom")
    tiles = far_block
    row_ids = far_row_ids
    col_ids = far_col_ids
    far_grads = select(
        "kqr,rbf->kqbf", membership_flags(row_ids, blocks_dom, jnp.bfloat16), cluster_block_list
    )
    terms = tile_product("kqab,kqaf->kqbf", tiles, far_grads)
    placed = precise_total_sum(
        "kqc,kqbf->kcbf", membership_flags(col_ids, blocks_per_processor, jnp.float32), terms
    )
    far_grad = lax.psum_scatter(
        placed.reshape(row_count, feat_width).astype(jnp.bfloat16),
        "dom",
        scatter_dimension=0,
        tiled=True,
    ).astype(jnp.float32)
    grad_features = far_grad + local_contribution.reshape(rows_dev, feat_width)
    return (hidden, grad_features, weight_grad)


def solution(mesh):
    placed = (
        P(("dom", "repl"), None),
        P(),
        P(),
        P(("dom", "repl"), None),
        P(("dom", "repl"), None, None),
        P(("dom", "repl"), None),
        P(("dom", "repl"), None),
        P(("dom", "repl"), None, None, None, None),
        P(("dom", "repl"), None, None),
        P(("dom", "repl"), None, None),
    )
    return jax.shard_map(
        on_device,
        mesh=mesh,
        in_specs=placed,
        out_specs=(P(("dom", "repl"), None), P(("dom", "repl"), None), P()),
        check_vma=False,
    )
```

profile of v0, /device:TPU:2, one launch (start us, length us, event | category | flops | bytes accessed | tf_op | source)
XLA Modules:
  0.0 674.9 jit_solution(15560080894403100846)
XLA Ops:
  7.2 1.9 convert_element_type.53
  9.2 1.5 convolution_convert_fusion.1
  10.7 1.9 convolution_bitcast_fusion.3
  12.6 2.3 copy.19
  15.0 0.1 convert_reduce_fusion
  15.2 3.6 fusion.28
  18.7 66.3 %all-gather.3.cloned.1.call-done = bf16[16384,256]{1,0:T(8,128)(2,1)} async-done(((bf16[512,256]{1,0:T(8,128)(2,1)}), bf16[16384,256]{1,0:T(8,128)(2,1)}) %all-gather.3.cloned.1.call-update) | async-done | bytes 8388624 | tf_op jit(solution)/shard_map/all_gather | solution.py:71
  85.0 11.8 %fusion = bf16[32,1,128,256]{3,1,2,0:T(2,128)(2,1)} fusion(bf16[32,4,128,256]{3,2,1,0:T(8,128)(2,1)} %bitcast.65, pred[32,4,1,1]{1,0,2,3:T(32,128)(4,1)S(1)} %get-tuple-element.6), kind=kOutput, calls=%fused_computation.1 | convolution fusion | flops 8388608 | bytes 10485888 | tf_op jit(solution)/shard_map/kqc,kcbf->kqbf/dot_general | solution.py:22
  96.8 8.6 %copy.31 = bf16[32,1,128,256]{2,3,0,1:T(8,128)(2,1)S(1)} copy(bf16[32,1,128,256]{3,1,2,0:T(2,128)(2,1)} %fusion) | data formatting | bytes 4194304 | tf_op jit(solution)/shard_map/kqc,kcbf->kqbf/dot_general | solution.py:22
  105.4 2.7 convolution_bitcast_fusion.1
  108.1 5.5 copy.20
  113.6 5.7 convolution_add_fusion
  119.3 4.4 copy.21
  123.8 89.6 %reduce-scatter.3.cloned.1.call-done = f32[512,256]{1,0:T(8,128)} async-done(((f32[4096,256]{1,0:T(8,128)}), f32[512,256]{1,0:T(8,128)}) %reduce-scatter.3.cloned.1.call-update) | async-done | bytes 524304 | tf_op jit(solution)/shard_map/reduce_scatter | solution.py:85
  213.4 2.2 multiply_convert_fusion.1
  215.7 1.0 convolution_convert_fusion.2
  216.7 0.2 all-reduce.2.cloned.1.call-start
  216.9 1.0 fusion.14
  218.0 57.9 %all-gather.5.cloned.1.call-done = bf16[4096,256]{1,0:T(8,128)(2,1)} async-done(((bf16[512,256]{1,0:T(8,128)(2,1)}), bf16[4096,256]{1,0:T(8,128)(2,1)}) %all-gather.5.cloned.1.call-update) | async-done | bytes 2097168 | tf_op jit(solution)/shard_map/all_gather | solution.py:97
  275.8 2.9 convolution_convert_fusion
  278.8 3.7 convolution_bitcast_fusion
  282.5 5.6 copy.24
  288.1 8.7 %multiply_convert_fusion = bf16[32,4,128,256]{3,2,1,0:T(8,128)(2,1)} fusion(f32[32,128,256]{2,1,0:T(8,128)} %copy.24, f32[32,4]{1,0:T(8,128)S(1)} %get-tuple-element.5), kind=kLoop, calls=%fused_computation | loop fusion | flops 8388608 | bytes 12583424 | tf_op jit(solution)/shard_map/convert_element_type | solution.py:122
  296.8 238.4 %all-reduce.2.cloned.1.call-done = f32[256,256]{1,0:T(8,128)} async-done(((f32[256,256]{1,0:T(8,128)}), f32[256,256]{1,0:T(8,128)}) %all-reduce.2.cloned.1.call-update) | async-done | bytes 262160 | tf_op jit(solution)/shard_map/psum | solution.py:99
  535.2 1.7 broadcast_multiply_fusion
  537.0 1.2 fusion.6
  538.2 0.5 convolution_bitcast_fusion.2
  538.7 2.0 copy.27
  540.8 2.4 fusion.33
  543.2 0.1 copy.28
  543.3 123.3 %reduce-scatter.5.cloned.1.call-done = bf16[512,256]{1,0:T(8,128)(2,1)} async-done(((bf16[16384,256]{1,0:T(8,128)(2,1)}), bf16[512,256]{1,0:T(8,128)(2,1)}) %reduce-scatter.5.cloned.1.call-update) | async-done | bytes 262160 | tf_op jit(solution)/shard_map/reduce_scatter | solution.py:121
  666.6 1.8 bitcast_add_fusion
  (35 shorter events, 0.4 us)
Async XLA Ops:
  7.2 98.3 %copy-start = (bf16[1,32,1,128,128]{4,3,2,1,0:T(8,128)(2,1)S(1)}, bf16[1,32,1,128,128]{4,3,2,1,0:T(8,128)(2,1)}, u32[]{:S(2)}) copy-start(bf16[1,32,1,128,128]{4,3,2,1,0:T(8,128)(2,1)} %param.17) | copy-start | bytes 3145732
  7.2 3.5 copy-start.2
  7.2 77.8 %all-gather.3.cloned.1.call-start = ((), (), s32[]{:S(2)}) async-start(), calls=%async_computation.2 | async-start | bytes 8650752 | tf_op jit(solution)/shard_map/all_gather | solution.py:71
  9.2 204.3 %reduce-scatter.3.cloned.1.call-start = ((), (), s32[]{:S(2)}) async-start(), calls=%async_computation.3 | async-start | bytes 4718592 | tf_op jit(solution)/shard_map/reduce_scatter | solution.py:85
  12.6 2.3 copy-start.11
  12.6 2.5 copy-start.8
  108.1 5.5 copy-start.6
  123.7 89.7 %copy-start.5 = (bf16[256,256]{1,0:T(8,128)(2,1)S(1)}, bf16[256,256]{1,0:T(8,128)(2,1)}, u32[]{:S(2)}) copy-start(bf16[256,256]{1,0:T(8,128)(2,1)} %param.11) | copy-start | bytes 393220
  123.7 89.7 %copy-start.9 = (bf16[512,256]{1,0:T(8,128)(2,1)S(1)}, bf16[512,256]{1,0:T(8,128)(2,1)}, u32[]{:S(2)}) copy-start(bf16[512,256]{1,0:T(8,128)(2,1)} %param.13) | copy-start | bytes 786436
  123.7 89.7 %copy-start.10 = (f32[256]{0:T(256)S(1)}, f32[256]{0:T(256)}, u32[]{:S(2)}) copy-start(f32[256]{0:T(256)} %param.12) | copy-start | bytes 3076
  123.7 152.1 %all-gather.5.cloned.1.call-start = ((), (), s32[]{:S(2)}) async-start(), calls=%async_computation.4 | async-start | bytes 2359296 | tf_op jit(solution)/shard_map/all_gather | solution.py:97
  213.4 3.5 copy-start.4
  216.7 318.5 %all-reduce.2.cloned.1.call-start = ((), (), s32[]{:S(2)}) async-start(), calls=%async_computation.6 | async-start | bytes 524288 | tf_op jit(solution)/shard_map/psum | solution.py:99
  217.9 448.7 %reduce-scatter.5.cloned.1.call-start = ((), (), s32[]{:S(2)}) async-start(), calls=%async_computation.5 | async-start | bytes 8650752 | tf_op jit(solution)/shard_map/reduce_scatter | solution.py:121
  296.8 240.1 %copy-start.1 = (bf16[4096,256]{1,0:T(8,128)(2,1)S(1)}, bf16[4096,256]{1,0:T(8,128)(2,1)}, u32[]{:S(2)}) copy-start(bf16[4096,256]{1,0:T(8,128)(2,1)} %all-gather.5.cloned.1.call-done) | copy-start | bytes 6291460
  535.2 3.0 copy-start.3
  538.7 2.0 copy-start.7
Sparse Core Ops, SparseCore 0:
  10.4 74.5 all-gather.2
  123.9 89.5 reduce-scatter.2
  216.8 59.0 all-gather.4
  281.7 253.4 all-reduce.1
  537.6 128.9 reduce-scatter.4
where the time goes:
time: 676 us; the launch traced here: 675 us
  waiting for transfers between devices  576 us (85%)
  matrix products  42.2 us (6%)
  local copies, waits for them, and re-layouts  28.6 us (4%)
  other arithmetic  14.4 us (2%)
  between operations  13.9 us (2%)
    psum x1, waiting for transfers between devices, on_device(): lax.psum(weight_term, ('dom', 'repl')) * (1.0 / math.sqrt(node_total))  238 us
    reduce_scatter x1, waiting for transfers between devices, on_device(): lax.psum_scatter(placed.reshape(row_count, feat_width).astype(jnp.bfloat1...  123 us
    reduce_scatter x1, waiting for transfers between devices, on_device(): lax.psum_scatter(group_partial, 'repl', scatter_dimension=0, tiled=True)  89.6 us
    all_gather x1, waiting for transfers between devices, on_device(): shard_rows = lax.all_gather(reduced, 'dom', axis=0, tiled=True)  66.3 us
    all_gather x1, waiting for transfers between devices, on_device(): group_grad = lax.all_gather(grad_rows, 'repl', axis=0, tiled=True)  57.9 us
    dot_general x4, matrix products, select(): jnp.einsum(form, hot, values, preferred_element_type=jnp.float32)  17.5 us
    dot_general x4, local copies, waits for them, and re-layouts, tile_product(): return jnp.einsum(form, tiles, values, preferred_element_type=jnp.float32)  15.4 us
  transfers between devices with their start and end apart: 5, of which 5 were waited for; matrix products, arithmetic and copies ran while one was open for 6% of the time, Pallas kernels for 0%

commit v1 on v0

--- a/solution.py
+++ b/solution.py
@@ -3,6 +3,9 @@
 import jax.numpy as jnp
 from jax import lax
 from jax.sharding import PartitionSpec as P
+from jax.lax import all_gather
+
+positions_produce = lambda frame_in: all_gather(frame_in, axis_name=("dom", "repl")).sum(axis=0)
 
 
 def membership_flags(index, extent, dtype):
@@ -96,7 +99,7 @@
     ).astype(jnp.bfloat16)
     group_grad = lax.all_gather(grad_rows, "repl", axis=0, tiled=True)
     node_total = rows_dev * dom_count * repl_count
-    weight_grad = lax.psum(weight_term, ("dom", "repl")) * (1.0 / math.sqrt(node_total))
+    weight_grad = positions_produce(weight_term) * (1.0 / math.sqrt(node_total))
     cluster_block_list = group_grad.reshape(blocks_dom, tile_size, feat_width)
     near_grads = select(
         "om,mgh->ogh", membership_flags(near_row_ids, blocks_dom, jnp.bfloat16), cluster_block_list

time: 676 us -> 1250 us (1.85)
  waiting for transfers between devices: 576 us -> 1120 us
  other arithmetic: 14.4 us -> 34.5 us
    all_gather x0 -> x1, waiting for transfers between devices: none -> 786 us  [all_gather(frame_in, axis_name=('dom', 'repl')).sum(axis=0)]
    psum x1 -> x0, waiting for transfers between devices: 238 us -> none  [on_device(): lax.psum(weight_term, ('dom', 'repl')) * (1.0 / math.sqrt(node_total))]
    reduce_sum x0 -> x1, other arithmetic: none -> 21.1 us  [all_gather(frame_in, axis_name=('dom', 'repl')).sum(axis=0)]
  transfers between devices with their start and end apart: 5 -> 5, of which waited for: 5 -> 5; matrix products, arithmetic and copies ran while one was open for 6% -> 2% of each run, Pallas kernels for 0% -> 0%
where the time goes in v1:
time: 1250 us; the launch traced here: 1240 us
  waiting for transfers between devices  1120 us (90%)
  matrix products  43.1 us (3%)
  other arithmetic  34.5 us (3%)
  local copies, waits for them, and re-layouts  29.5 us (2%)
  between operations  13.9 us (1%)
    all_gather x1, waiting for transfers between devices, all_gather(frame_in, axis_name=('dom', 'repl')).sum(axis=0)  786 us
    reduce_scatter x1, waiting for transfers between devices, on_device(): lax.psum_scatter(placed.reshape(row_count, feat_width).astype(jnp.bfloat1...  120 us
    reduce_scatter x1, waiting for transfers between devices, on_device(): lax.psum_scatter(group_partial, 'repl', scatter_dimension=0, tiled=True)  89.7 us
    all_gather x1, waiting for transfers between devices, on_device(): shard_rows = lax.all_gather(reduced, 'dom', axis=0, tiled=True)  66.3 us
    all_gather x1, waiting for transfers between devices, on_device(): group_grad = lax.all_gather(grad_rows, 'repl', axis=0, tiled=True)  59 us
  transfers between devices with their start and end apart: 5, of which 5 were waited for; matrix products, arithmetic and copies ran while one was open for 2% of the time, Pallas kernels for 0%

profile of v1, /device:TPU:2, one launch (start us, length us, event | category | flops | bytes accessed | tf_op | source)
XLA Modules:
  0.0 1242.0 jit_solution(6981419942553817055)
XLA Ops:
  7.2 1.9 convert_element_type.53
  9.2 1.5 convolution_convert_fusion.1
  10.7 1.9 convolution_bitcast_fusion.3
  12.6 2.3 copy.19
  15.2 3.6 fusion.28
  18.7 66.3 %all-gather.5.cloned.1.call-done = bf16[16384,256]{1,0:T(8,128)(2,1)} async-done(((bf16[512,256]{1,0:T(8,128)(2,1)}), bf16[16384,256]{1,0:T(8,128)(2,1)}) %all-gather.5.cloned.1.call-update) | async-done | bytes 8388624 | tf_op jit(solution)/shard_map/all_gather | solution.py:74
  85.0 11.8 fusion
  96.8 8.6 copy.31
  105.4 2.7 convolution_bitcast_fusion.1
  108.1 5.5 copy.20
  113.6 5.7 convolution_add_fusion
  119.3 4.4 copy.21
  123.8 89.7 %reduce-scatter.3.cloned.1.call-done = f32[512,256]{1,0:T(8,128)} async-done(((f32[4096,256]{1,0:T(8,128)}), f32[512,256]{1,0:T(8,128)}) %reduce-scatter.3.cloned.1.call-update) | async-done | bytes 524304 | tf_op jit(solution)/shard_map/reduce_scatter | solution.py:88
  213.5 2.2 multiply_convert_fusion.1
  215.6 1.0 convolution_convert_fusion.2
  216.6 0.2 reduce-scatter.5.cloned.1.call-start
  216.8 59.0 %all-gather.7.cloned.1.call-done = bf16[4096,256]{1,0:T(8,128)(2,1)} async-done(((bf16[512,256]{1,0:T(8,128)(2,1)}), bf16[4096,256]{1,0:T(8,128)(2,1)}) %all-gather.7.cloned.1.call-update) | async-done | bytes 2097168 | tf_op jit(solution)/shard_map/all_gather | solution.py:100
  275.8 2.9 convolution_convert_fusion
  278.7 3.7 convolution_bitcast_fusion
  282.5 5.6 copy.24
  288.1 8.7 multiply_convert_fusion
  296.9 1.0 copy-done.4
  297.8 1.0 fusion.14
  298.9 1.2 fusion.6
  300.1 1.6 convolution_bitcast_fusion.2
  301.7 2.0 copy.27
  303.7 2.4 fusion.33
  306.2 120.1 %reduce-scatter.5.cloned.1.call-done = bf16[512,256]{1,0:T(8,128)(2,1)} async-done(((bf16[16384,256]{1,0:T(8,128)(2,1)}), bf16[512,256]{1,0:T(8,128)(2,1)}) %reduce-scatter.5.cloned.1.call-update) | async-done | bytes 262160 | tf_op jit(solution)/shard_map/reduce_scatter | solution.py:124
  426.3 1.8 bitcast_add_fusion
  428.1 785.6 %all-gather.9.cloned.1.call-done = f32[65536,256]{1,0:T(8,128)} async-done(((f32[256,256]{1,0:T(8,128)}), f32[65536,256]{1,0:T(8,128)}) %all-gather.9.cloned.1.call-update) | async-done | bytes 67108880 | tf_op jit(solution)/shard_map/all_gather | solution.py:8
  1213.7 21.1 %reduce_sum.19 = f32[256,256]{1,0:T(8,128)S(1)} reduce(f32[256,256,256]{2,1,0:T(8,128)} %bitcast.22, f32[]{:T(128)} %constant.2.clone.1), dimensions={0}, to_apply=%region_3.4 | reduce | flops 16711680 | bytes 67371008 | tf_op jit(solution)/shard_map/reduce_sum | solution.py:8
  1234.8 0.7 broadcast_multiply_fusion
  (36 shorter events, 0.7 us)
Async XLA Ops:
  7.2 98.3 %copy-start = (bf16[1,32,1,128,128]{4,3,2,1,0:T(8,128)(2,1)S(1)}, bf16[1,32,1,128,128]{4,3,2,1,0:T(8,128)(2,1)}, u32[]{:S(2)}) copy-start(bf16[1,32,1,128,128]{4,3,2,1,0:T(8,128)(2,1)} %param.17) | copy-start | bytes 3145732
  7.2 3.5 copy-start.3
  7.2 77.8 %all-gather.5.cloned.1.call-start = ((), (), s32[]{:S(2)}) async-start(), calls=%async_computation.2 | async-start | bytes 8650752 | tf_op jit(solution)/shard_map/all_gather | solution.py:74
  9.2 204.3 %reduce-scatter.3.cloned.1.call-start = ((), (), s32[]{:S(2)}) async-start(), calls=%async_computation.3 | async-start | bytes 4718592 | tf_op jit(solution)/shard_map/reduce_scatter | solution.py:88
  12.6 2.3 copy-start.11
  12.6 2.5 copy-start.8
  108.1 5.5 copy-start.6
  123.7 89.7 %copy-start.5 = (bf16[256,256]{1,0:T(8,128)(2,1)S(1)}, bf16[256,256]{1,0:T(8,128)(2,1)}, u32[]{:S(2)}) copy-start(bf16[256,256]{1,0:T(8,128)(2,1)} %param.11) | copy-start | bytes 393220
  123.7 89.7 %copy-start.9 = (bf16[512,256]{1,0:T(8,128)(2,1)S(1)}, bf16[512,256]{1,0:T(8,128)(2,1)}, u32[]{:S(2)}) copy-start(bf16[512,256]{1,0:T(8,128)(2,1)} %param.13) | copy-start | bytes 786436
  123.7 89.7 %copy-start.10 = (f32[256]{0:T(256)S(1)}, f32[256]{0:T(256)}, u32[]{:S(2)}) copy-start(f32[256]{0:T(256)} %param.12) | copy-start | bytes 3076
  123.7 152.1 %all-gather.7.cloned.1.call-start = ((), (), s32[]{:S(2)}) async-start(), calls=%async_computation.4 | async-start | bytes 2359296 | tf_op jit(solution)/shard_map/all_gather | solution.py:100
  216.6 209.7 %reduce-scatter.5.cloned.1.call-start = ((), (), s32[]{:S(2)}) async-start(), calls=%async_computation.5 | async-start | bytes 8650752 | tf_op jit(solution)/shard_map/reduce_scatter | solution.py:124
  296.8 1.0 copy-start.4
  296.8 2.0 copy-start.2
  296.8 916.8 %all-gather.9.cloned.1.call-start = ((), (), s32[]{:S(2)}) async-start(), calls=%async_computation.6 | async-start | bytes 67371008 | tf_op jit(solution)/shard_map/all_gather | solution.py:8
  301.7 2.0 copy-start.7
  1213.7 21.8 %copy-start.1 = (bf16[1,32,1,128,128]{4,3,2,1,0:T(8,128)(2,1)S(1)}, bf16[1,32,1,128,128]{4,3,2,1,0:T(8,128)(2,1)}, u32[]{:S(2)}) copy-start(bf16[1,32,1,128,128]{4,3,2,1,0:T(8,128)(2,1)} %param.17) | copy-start | bytes 3145732
Sparse Core Ops, SparseCore 0:
  10.4 74.5 all-gather.4
  123.9 89.5 reduce-scatter.2
  216.7 59.0 all-gather.6
  297.0 129.2 reduce-scatter.4
  428.6 785.0 all-gather.8
